TPU v7x, 32 devices: a whole 2x2x4 slice. The times are simulated.
32 devices in a mesh: dp: 16 (over z, y, x), mp: 2 (over core).
Axes of the slice: x: 2, y: 2, z: 4, core: 2. Of those that a mesh axis runs over, the one named last changes fastest.
Arguments:
- tokens: bfloat16 [16384, 768], P('dp'), may hold values from -6 to 6
- cotangent: bfloat16 [16384, 768], P('dp'), may hold values from -6 to 6
- seg_lengths: int32 [32, 8], P('dp'), may hold values from 1 to 256, 512 in all within a row
- pad_counts: int32 [32], P('dp'), may hold values from 0 to 64
- qkv_weight: float32 [3, 768, 768], P(None, 'dp', 'mp'), may hold values from -0.3125 to 0.3125
- first_qkv: float32 [3, 768, 768], P(None, 'dp', 'mp'), may hold values from -0.00024414062 to 0.00024414062
- second_qkv: float32 [3, 768, 768], P(None, 'dp', 'mp'), may hold values from 7.4315953e-09 to 2.974051e-08
- average_qkv: float32 [3, 768, 768], P(None, 'dp', 'mp'), may hold values from -0.3125 to 0.3125
- attn_weight: float32 [768, 768], P(('mp', 'dp')), may hold values from -0.625 to 0.625
- first_attn: float32 [768, 768], P(('mp', 'dp')), may hold values from -0.00024414062 to 0.00024414062
- second_attn: float32 [768, 768], P(('mp', 'dp')), may hold values from 7.4315953e-09 to 2.974051e-08
- average_attn: float32 [768, 768], P(('mp', 'dp')), may hold values from -0.625 to 0.625
- up_weight: float32 [768, 3072], P('dp', 'mp'), may hold values from -0.21875 to 0.21875
- first_up: float32 [768, 3072], P('dp', 'mp'), may hold values from -0.00024414062 to 0.00024414062
- second_up: float32 [768, 3072], P('dp', 'mp'), may hold values from 7.4315953e-09 to 2.974051e-08
- average_up: float32 [768, 3072], P('dp', 'mp'), may hold values from -0.21875 to 0.21875
- down_weight: float32 [3072, 768], P(('mp', 'dp')), may hold values from -0.109375 to 0.109375
- first_down: float32 [3072, 768], P(('mp', 'dp')), may hold values from -0.00024414062 to 0.00024414062
- second_down: float32 [3072, 768], P(('mp', 'dp')), may hold values from 7.4315953e-09 to 2.974051e-08
- average_down: float32 [3072, 768], P(('mp', 'dp')), may hold values from -0.109375 to 0.109375
- head_bias: float32 [2, 768], P(None, ('mp', 'dp')), may hold values from -1.75 to 1.75
- first_head: float32 [2, 768], P(None, ('mp', 'dp')), may hold values from -0.00048828125 to 0.00048828125
- second_head: float32 [2, 768], P(None, ('mp', 'dp')), may hold values from 2.974051e-08 to 1.1896204e-07
- average_head: float32 [2, 768], P(None, ('mp', 'dp')), may hold values from -1.75 to 1.75
- hidden_bias: float32 [3072], P(('mp', 'dp')), may hold values from -1.75 to 1.75
- first_hidden: float32 [3072], P(('mp', 'dp')), may hold values from -0.00015258789 to 0.00015258789
- second_hidden: float32 [3072], P(('mp', 'dp')), may hold values from 3.306071e-09 to 1.3224284e-08
- average_hidden: float32 [3072], P(('mp', 'dp')), may hold values from -1.75 to 1.75
- layer_vectors: float32 [6, 768], P(None, 'dp'), may hold values from -0.8 to 2.4
- first_vectors: float32 [6, 768], P(None, 'dp'), may hold values from -0.00048828125 to 0.00048828125
- second_vectors: float32 [6, 768], P(None, 'dp'), may hold values from 2.974051e-08 to 1.1896204e-07
- average_vectors: float32 [6, 768], P(None, 'dp'), may hold values from -3 to 3
Outputs:
- layer_output: bfloat16 [16384, 768], P('dp')
- input_grad: float32 [16384, 768], P('dp')
- grad_norm: float32 [], replicated
- moment_qkv: float32 [3, 768, 768], P(None, 'dp', 'mp')
- square_qkv: float32 [3, 768, 768], P(None, 'dp', 'mp')
- updated_qkv: float32 [3, 768, 768], P(None, 'dp', 'mp')
- smooth_qkv: float32 [3, 768, 768], P(None, 'dp', 'mp')
- moment_attn: float32 [768, 768], P(('mp', 'dp'))
- square_attn: float32 [768, 768], P(('mp', 'dp'))
- updated_attn: float32 [768, 768], P(('mp', 'dp'))
- smooth_attn: float32 [768, 768], P(('mp', 'dp'))
- moment_up: float32 [768, 3072], P('dp', 'mp')
- square_up: float32 [768, 3072], P('dp', 'mp')
- updated_up: float32 [768, 3072], P('dp', 'mp')
- smooth_up: float32 [768, 3072], P('dp', 'mp')
- moment_down: float32 [3072, 768], P(('mp', 'dp'))
- square_down: float32 [3072, 768], P(('mp', 'dp'))
- updated_down: float32 [3072, 768], P(('mp', 'dp'))
- smooth_down: float32 [3072, 768], P(('mp', 'dp'))
- moment_head: float32 [2, 768], P(None, ('mp', 'dp'))
- square_head: float32 [2, 768], P(None, ('mp', 'dp'))
- updated_head: float32 [2, 768], P(None, ('mp', 'dp'))
- smooth_head: float32 [2, 768], P(None, ('mp', 'dp'))
- moment_hidden: float32 [3072], P(('mp', 'dp'))
- square_hidden: float32 [3072], P(('mp', 'dp'))
- updated_hidden: float32 [3072], P(('mp', 'dp'))
- smooth_hidden: float32 [3072], P(('mp', 'dp'))
- moment_vectors: float32 [6, 768], P(None, 'dp')
- square_vectors: float32 [6, 768], P(None, 'dp')
- updated_vectors: float32 [6, 768], P(None, 'dp')
- smooth_vectors: float32 [6, 768], P(None, 'dp')
All inputs are finite; a program needn't handle non-finite values.
Results may differ from a plain program's by a relative error of at most 0.015.
The roundings to bfloat16 on the way count: a program that leaves them out, or rounds other values in their place, can miss the bound.
Values may be sent and summed in bfloat16 or wider, within the bound.
No kernel may reach another device: no remote copies, remote signals or barrier semaphores. Data moves between devices by JAX's collectives and lax.ppermute only.
A program may use at most 192 MiB of HBM per device.

v0:
```python
import jax
import jax.numpy as jnp
from jax import lax
from jax.sharding import PartitionSpec as P

HD = 64
SEQ = 512
STEP = 7
NORM_EPS = 1e-05
SCORE_SCALE = 0.125
LEARN_RATE = 0.03
VECTOR_RATE = 0.4
BETA_ONE = 0.9
BETA_TWO = 0.95
ADAM_EPS = 1e-08
WEIGHT_DECAY = 0.1
EMA_RATE = 0.8
CLIP_NORM = 1.0
GELU_COEF = 0.7978845608028654


def gelu_tanh(value):
    return 0.5 * value * (1.0 + jnp.tanh(GELU_COEF * (value + 0.044715 * value * value * value)))


def norm_parts(rows):
    row_mean = jnp.mean(rows, axis=1, keepdims=True)
    centered = rows - row_mean
    inv_std = lax.rsqrt(jnp.mean(centered * centered, axis=1, keepdims=True) + NORM_EPS)
    return (centered * inv_std, inv_std)


def norm_back(grad_in, normed, inv_std, gain):
    scaled = grad_in * gain
    return inv_std * (
        scaled
        - jnp.mean(scaled, axis=1, keepdims=True)
        - normed * jnp.mean(scaled * normed, axis=1, keepdims=True)
    )


def visible_keys(lengths, padding):
    position = jnp.arange(SEQ, dtype=jnp.int32)
    bounds = jnp.cumsum(lengths)
    segment = jnp.sum((position[:, None] >= bounds[None, :]).astype(jnp.int32), axis=1)
    padded = position >= SEQ - padding
    same_segment = segment[:, None] == segment[None, :]
    itself = position[:, None] == position[None, :]
    return same_segment & (jnp.logical_not(padded)[None, :] | itself)


def kept_rows(padding):
    position = jnp.arange(SEQ, dtype=jnp.int32)
    return (position < SEQ - padding).astype(jnp.float32)


def split_heads(rows):
    return rows.reshape(SEQ, rows.shape[1] // HD, HD)


def masked_scores(query_heads, key_heads, allowed):
    scores = (
        jnp.einsum("qhe,khe->hqk", query_heads, key_heads, preferred_element_type=jnp.float32)
        * SCORE_SCALE
    )
    return jnp.where(allowed[None, :, :], scores, -1e30)


def attend_forward(packed):
    queries, key_rows, value_rows, allowed = packed
    value_heads = split_heads(value_rows)
    scores = masked_scores(split_heads(queries), split_heads(key_rows), allowed)
    row_max = jnp.max(scores, axis=2, keepdims=True)
    exponent = jnp.exp(scores - row_max)
    row_sum = jnp.sum(exponent, axis=2, keepdims=True)
    probs = (exponent / row_sum).astype(jnp.bfloat16)
    mixed = jnp.einsum("hqk,khe->qhe", probs, value_heads, preferred_element_type=jnp.float32)
    return (mixed.reshape(SEQ, -1).astype(jnp.bfloat16), (row_max + jnp.log(row_sum))[:, :, 0])


def attend_backward(packed):
    queries, key_rows, value_rows, allowed, log_total, grad_mixed = packed
    query_heads = split_heads(queries)
    key_heads = split_heads(key_rows)
    value_heads = split_heads(value_rows)
    scores = masked_scores(query_heads, key_heads, allowed)
    probs = jnp.exp(scores - log_total[:, :, None])
    grad_heads = split_heads(grad_mixed)
    grad_probs = jnp.einsum(
        "qhe,khe->hqk", grad_heads, value_heads, preferred_element_type=jnp.float32
    )
    row_dot = jnp.sum(probs * grad_probs, axis=2, keepdims=True)
    grad_scores = (probs * (grad_probs - row_dot)).astype(jnp.bfloat16)
    grad_query = (
        jnp.einsum("hqk,khe->qhe", grad_scores, key_heads, preferred_element_type=jnp.float32)
        * SCORE_SCALE
    )
    grad_key = (
        jnp.einsum("hqk,qhe->khe", grad_scores, query_heads, preferred_element_type=jnp.float32)
        * SCORE_SCALE
    )
    grad_value = jnp.einsum(
        "hqk,qhe->khe", probs.astype(jnp.bfloat16), grad_heads, preferred_element_type=jnp.float32
    )
    return jnp.stack(
        [grad_query.reshape(SEQ, -1), grad_key.reshape(SEQ, -1), grad_value.reshape(SEQ, -1)],
        axis=0,
    )


def adam_step(gradient, master, first, second, average, factor, decay_rate, step_rate):
    clipped = gradient * factor
    first_new = BETA_ONE * first + (1.0 - BETA_ONE) * clipped
    second_new = BETA_TWO * second + (1.0 - BETA_TWO) * clipped * clipped
    first_hat = first_new / (1.0 - BETA_ONE**STEP)
    second_hat = second_new / (1.0 - BETA_TWO**STEP)
    master_new = master - step_rate * (
        first_hat / (jnp.sqrt(second_hat) + ADAM_EPS) + decay_rate * master
    )
    average_new = EMA_RATE * average + (1.0 - EMA_RATE) * master_new
    return (first_new, second_new, master_new, average_new)


def body(
    tokens,
    cotangent,
    seg_lengths,
    pad_counts,
    qkv_weight,
    first_qkv,
    second_qkv,
    average_qkv,
    attn_weight,
    first_attn,
    second_attn,
    average_attn,
    up_weight,
    first_up,
    second_up,
    average_up,
    down_weight,
    first_down,
    second_down,
    average_down,
    head_bias,
    first_head,
    second_head,
    average_head,
    hidden_bias,
    first_hidden,
    second_hidden,
    average_hidden,
    layer_vectors,
    first_vectors,
    second_vectors,
    average_vectors,
):
    bfloat = jnp.bfloat16
    single = jnp.float32
    shared = (
        lax.all_gather(qkv_weight.astype(bfloat), "dp", axis=1, tiled=True),
        lax.all_gather(attn_weight.astype(bfloat), "dp", axis=0, tiled=True),
        lax.all_gather(up_weight.astype(bfloat), "dp", axis=0, tiled=True),
        lax.all_gather(down_weight.astype(bfloat), "dp", axis=0, tiled=True),
        lax.all_gather(head_bias.astype(bfloat), "dp", axis=1, tiled=True),
        lax.all_gather(hidden_bias.astype(bfloat), "dp", axis=0, tiled=True),
        lax.all_gather(layer_vectors.astype(bfloat), "dp", axis=1, tiled=True),
    )
    qkv_mat, attn_mat, up_mat, down_mat = (shared[0], shared[1], shared[2], shared[3])
    head_vec = shared[4].astype(single)
    hidden_vec = shared[5].astype(single)
    layer_vec = shared[6].astype(single)
    row_count = tokens.shape[0]
    seq_here = row_count // SEQ
    local_width = qkv_mat.shape[2]
    shaped = (seq_here, SEQ, local_width)
    allowed = jax.vmap(visible_keys)(seg_lengths, pad_counts)
    kept = jax.vmap(kept_rows)(pad_counts).reshape(row_count, 1)
    rows = tokens.astype(single)
    normed_one, inv_one = norm_parts(rows)
    first_in = (normed_one * layer_vec[0] + layer_vec[1]).astype(bfloat)
    projected = jnp.einsum("td,kdc->ktc", first_in, qkv_mat, preferred_element_type=single)
    queries = (projected[0] + head_vec[0]).astype(bfloat)
    key_rows = projected[1].astype(bfloat)
    value_rows = (projected[2] + head_vec[1]).astype(bfloat)
    mixed, log_total = lax.map(
        attend_forward,
        (queries.reshape(shaped), key_rows.reshape(shaped), value_rows.reshape(shaped), allowed),
    )
    mixed = mixed.reshape(row_count, local_width)
    attn_part = jnp.dot(mixed, attn_mat, preferred_element_type=single)
    hidden_one = (
        rows + lax.psum(attn_part.astype(jnp.bfloat16), "mp").astype(jnp.float32) + layer_vec[4]
    )
    normed_two, inv_two = norm_parts(hidden_one)
    second_in = (normed_two * layer_vec[2] + layer_vec[3]).astype(bfloat)
    pre_act = jnp.dot(second_in, up_mat, preferred_element_type=single) + hidden_vec
    act_value, act_pull = jax.vjp(gelu_tanh, pre_act)
    activated = act_value.astype(bfloat)
    down_part = jnp.dot(activated, down_mat, preferred_element_type=single)
    layer_output = (
        hidden_one
        + lax.psum(down_part.astype(jnp.bfloat16), "mp").astype(jnp.float32)
        + layer_vec[5]
    ).astype(bfloat)
    grad_out = cotangent.astype(single) * kept
    grad_out_low = grad_out.astype(bfloat)
    grad_down = jnp.einsum("tf,td->fd", activated, grad_out_low, preferred_element_type=single)
    grad_act = jnp.einsum("td,fd->tf", grad_out_low, down_mat, preferred_element_type=single)
    grad_pre = act_pull(grad_act)[0]
    grad_hidden = jnp.sum(grad_pre, axis=0)
    grad_pre_low = grad_pre.astype(bfloat)
    grad_up = jnp.einsum("td,tf->df", second_in, grad_pre_low, preferred_element_type=single)
    second_part = jnp.einsum("tf,df->td", grad_pre_low, up_mat, preferred_element_type=single)
    grad_second = lax.psum(second_part.astype(jnp.bfloat16), "mp").astype(jnp.float32)
    grad_hidden_one = grad_out + norm_back(grad_second, normed_two, inv_two, layer_vec[2])
    grad_hidden_low = grad_hidden_one.astype(bfloat)
    grad_attn = jnp.einsum("tc,td->cd", mixed, grad_hidden_low, preferred_element_type=single)
    grad_mixed = jnp.einsum(
        "td,cd->tc", grad_hidden_low, attn_mat, preferred_element_type=single
    ).astype(bfloat)
    grad_proj = lax.map(
        attend_backward,
        (
            queries.reshape(shaped),
            key_rows.reshape(shaped),
            value_rows.reshape(shaped),
            allowed,
            log_total,
            grad_mixed.reshape(shaped),
        ),
    )
    grad_proj = jnp.transpose(grad_proj, (1, 0, 2, 3)).reshape(3, row_count, local_width)
    grad_head = jnp.stack([jnp.sum(grad_proj[0], axis=0), jnp.sum(grad_proj[2], axis=0)], axis=0)
    proj_low = grad_proj.astype(bfloat)
    grad_qkv = jnp.einsum("td,ktc->kdc", first_in, proj_low, preferred_element_type=single)
    first_part = jnp.einsum("ktc,kdc->td", proj_low, qkv_mat, preferred_element_type=single)
    grad_first = lax.psum(first_part.astype(jnp.bfloat16), "mp").astype(jnp.float32)
    input_grad = grad_hidden_one + norm_back(grad_first, normed_one, inv_one, layer_vec[0])
    grad_vectors = jnp.stack(
        [
            jnp.sum(grad_first * normed_one, axis=0),
            jnp.sum(grad_first, axis=0),
            jnp.sum(grad_second * normed_two, axis=0),
            jnp.sum(grad_second, axis=0),
            jnp.sum(grad_hidden_one, axis=0),
            jnp.sum(grad_out, axis=0),
        ],
        axis=0,
    )
    reduced = (
        lax.psum_scatter(grad_qkv, "dp", scatter_dimension=1, tiled=True),
        lax.psum_scatter(grad_attn, "dp", scatter_dimension=0, tiled=True),
        lax.psum_scatter(grad_up, "dp", scatter_dimension=0, tiled=True),
        lax.psum_scatter(grad_down, "dp", scatter_dimension=0, tiled=True),
        lax.psum_scatter(grad_head, "dp", scatter_dimension=1, tiled=True),
        lax.psum_scatter(grad_hidden, "dp", scatter_dimension=0, tiled=True),
        lax.psum_scatter(grad_vectors, "dp", scatter_dimension=1, tiled=True),
    )
    squares_local = sum((jnp.sum(member * member) for member in reduced[:6])) + 0.5 * jnp.sum(
        reduced[6] * reduced[6]
    )
    grad_norm = jnp.sqrt(lax.psum(squares_local, ("dp", "mp")))
    factor = CLIP_NORM / jnp.maximum(grad_norm, CLIP_NORM)
    moment_qkv, square_qkv, updated_qkv, smooth_qkv = adam_step(
        reduced[0], qkv_weight, first_qkv, second_qkv, average_qkv, factor, WEIGHT_DECAY, LEARN_RATE
    )
    moment_attn, square_attn, updated_attn, smooth_attn = adam_step(
        reduced[1],
        attn_weight,
        first_attn,
        second_attn,
        average_attn,
        factor,
        WEIGHT_DECAY,
        LEARN_RATE,
    )
    moment_up, square_up, updated_up, smooth_up = adam_step(
        reduced[2], up_weight, first_up, second_up, average_up, factor, WEIGHT_DECAY, LEARN_RATE
    )
    moment_down, square_down, updated_down, smooth_down = adam_step(
        reduced[3],
        down_weight,
        first_down,
        second_down,
        average_down,
        factor,
        WEIGHT_DECAY,
        LEARN_RATE,
    )
    moment_head, square_head, updated_head, smooth_head = adam_step(
        reduced[4], head_bias, first_head, second_head, average_head, factor, 0.0, VECTOR_RATE
    )
    moment_hidden, square_hidden, updated_hidden, smooth_hidden = adam_step(
        reduced[5],
        hidden_bias,
        first_hidden,
        second_hidden,
        average_hidden,
        factor,
        0.0,
        VECTOR_RATE,
    )
    moment_vectors, square_vectors, updated_vectors, smooth_vectors = adam_step(
        reduced[6],
        layer_vectors,
        first_vectors,
        second_vectors,
        average_vectors,
        factor,
        0.0,
        VECTOR_RATE,
    )
    return (
        layer_output,
        input_grad,
        grad_norm,
        moment_qkv,
        square_qkv,
        updated_qkv,
        smooth_qkv,
        moment_attn,
        square_attn,
        updated_attn,
        smooth_attn,
        moment_up,
        square_up,
        updated_up,
        smooth_up,
        moment_down,
        square_down,
        updated_down,
        smooth_down,
        moment_head,
        square_head,
        updated_head,
        smooth_head,
        moment_hidden,
        square_hidden,
        updated_hidden,
        smooth_hidden,
        moment_vectors,
        square_vectors,
        updated_vectors,
        smooth_vectors,
    )


def solution(mesh):
    placed = (
        P("dp", None),
        P("dp", None),
        P("dp", None),
        P("dp"),
        P(None, "dp", "mp"),
        P(None, "dp", "mp"),
        P(None, "dp", "mp"),
        P(None, "dp", "mp"),
        P(("mp", "dp"), None),
        P(("mp", "dp"), None),
        P(("mp", "dp"), None),
        P(("mp", "dp"), None),
        P("dp", "mp"),
        P("dp", "mp"),
        P("dp", "mp"),
        P("dp", "mp"),
        P(("mp", "dp"), None),
        P(("mp", "dp"), None),
        P(("mp", "dp"), None),
        P(("mp", "dp"), None),
        P(None, ("mp", "dp")),
        P(None, ("mp", "dp")),
        P(None, ("mp", "dp")),
        P(None, ("mp", "dp")),
        P(("mp", "dp")),
        P(("mp", "dp")),
        P(("mp", "dp")),
        P(("mp", "dp")),
        P(None, "dp"),
        P(None, "dp"),
        P(None, "dp"),
        P(None, "dp"),
    )
    return jax.shard_map(
        body,
        mesh=mesh,
        in_specs=placed,
        out_specs=(
            P("dp", None),
            P("dp", None),
            P(),
            P(None, "dp", "mp"),
            P(None, "dp", "mp"),
            P(None, "dp", "mp"),
            P(None, "dp", "mp"),
            P(("mp", "dp"), None),
            P(("mp", "dp"), None),
            P(("mp", "dp"), None),
            P(("mp", "dp"), None),
            P("dp", "mp"),
            P("dp", "mp"),
            P("dp", "mp"),
            P("dp", "mp"),
            P(("mp", "dp"), None),
            P(("mp", "dp"), None),
            P(("mp", "dp"), None),
            P(("mp", "dp"), None),
            P(None, ("mp", "dp")),
            P(None, ("mp", "dp")),
            P(None, ("mp", "dp")),
            P(None, ("mp", "dp")),
            P(("mp", "dp")),
            P(("mp", "dp")),
            P(("mp", "dp")),
            P(("mp", "dp")),
            P(None, "dp"),
            P(None, "dp"),
            P(None, "dp"),
            P(None, "dp"),
        ),
        check_vma=False,
    )
```

profile of v0, /device:TPU:0, one launch (start us, length us, event | category | flops | bytes accessed | tf_op | source)
XLA Modules:
  0.0 1236.6 jit_solution(2257658814909541547)
XLA Ops:
  7.3 1.7 convert_element_type.145
  10.6 42.2 %all-gather.1 = bf16[16,24,2]{1,2,0:T(2,128)(2,1)S(1)} all-gather(bf16[1,24,2]{1,2,0:T(2,128)(2,1)S(1)} %convert_bitcast_fusion.1), channel_id=1, replica_groups=mesh['dp'=16,'mp'=2] {'dp'}, dimensions={0}, use_global_device_ids=true | all-gather | bytes 1632 | tf_op jit(solution)/shard_map/all_gather | solution.py:165
  53.6 35.9 %all-gather = bf16[16,48,6]{1,2,0:T(8,128)(2,1)S(1)} all-gather(bf16[1,48,6]{1,2,0:T(8,128)(2,1)S(1)} %convert_bitcast_fusion), channel_id=1, replica_groups=mesh['dp'=16,'mp'=2] {'dp'}, dimensions={0}, use_global_device_ids=true | all-gather | bytes 9792 | tf_op jit(solution)/shard_map/all_gather | solution.py:167
  91.8 1.7 convert_reduce_fusion.2
  96.2 43.5 %all_gather.24 = bf16[384,768]{1,0:T(8,128)(2,1)} all-gather(bf16[24,768]{1,0:T(8,128)(2,1)S(1)} %convert_element_type.152), channel_id=1, replica_groups=mesh['dp'=16,'mp'=2] {'dp'}, dimensions={0}, use_global_device_ids=true | all-gather | bytes 626688 | tf_op jit(solution)/shard_map/all_gather | solution.py:162
  139.8 4.0 convolution_bitcast_fusion
  146.1 3.0 copy.160
  149.2 1.6 copy.159
  152.2 3.0 add_convert_fusion.2
  155.2 19.9 %while.22 = (s32[]{:T(128)}, bf16[2,512,384]{2,1,0:T(8,128)(2,1)}, f32[2,6,512]{2,1,0:T(8,128)}, bf16[2,512,384]{1,2,0:T(8,128)(2,1)}, pred[2,512,512]{1,2,0:T(8...) while((s32[]{:T(128)}, bf16[2,512,384]{2,1,0:T(8,128)(2,1)}, ...), condition=%wide.region_7.8_spmd, body=%wide.region_4.7_spmd.sunk | while | flops 421721088 | bytes 25997480 | solution.py:186
  159.8 2.7 fusion.130
  169.7 2.7 fusion.130
  175.1 4.0 convolution_convert_fusion
  179.9 1.7 convert_element_type.160
  183.2 36.7 %all-reduce = bf16[1536]{0:T(1024)(128)(2,1)S(1)} all-reduce(bf16[1536]{0:T(1024)(128)(2,1)S(1)} %dynamic-update-slice), channel_id=1, replica_groups=mesh['dp'=16,'mp'=2] {'dp'}, use_global_device_ids=true, to_apply=%add | all-reduce | flops 1536 | bytes 6144
  220.6 2.1 fusion.47
  223.6 39.2 %all-gather.8.cloned.1.call-done = bf16[768,1536]{1,0:T(8,128)(2,1)} async-done(((bf16[48,1536]{1,0:T(8,128)(2,1)}), bf16[768,1536]{1,0:T(8,128)(2,1)}) %all-gather.8.cloned.1.call-update) | async-done | bytes 2359312 | tf_op jit(solution)/shard_map/all_gather | solution.py:163
  262.8 6.6 fusion.67
  269.4 58.1 %all-gather.10.cloned.1.call-done = bf16[1536,768]{1,0:T(8,128)(2,1)} async-done(((bf16[96,768]{1,0:T(8,128)(2,1)}), bf16[1536,768]{1,0:T(8,128)(2,1)}) %all-gather.10.cloned.1.call-update) | async-done | bytes 2359312 | tf_op jit(solution)/shard_map/all_gather | solution.py:164
  327.5 11.1 fusion.79
  338.6 1.7 copy-done.46
  340.3 3.7 convolution_convert_fusion.1
  344.1 8.6 convolution_convert_fusion.2
  352.7 10.7 all-reduce.13.cloned.1.call-done
  363.4 3.5 fusion.39
  367.0 3.4 fusion.75
  370.4 3.0 convolution_convert_fusion.3
  373.4 35.6 %while.23 = (s32[]{:T(128)}, f32[2,3,512,384]{3,2,0,1:T(8,128)}, bf16[2,512,384]{1,2,0:T(8,128)(2,1)S(1)}, pred[2,512,512]{1,2,0:T(8,128)(4,1)}, bf16[2,512,384]...) while((s32[]{:T(128)}, f32[2,3,512,384]{3,2,0,1:T(8,128)}, ...), condition=%wide.region_17.18_spmd, body=%wide.region_15.17_spmd.sunk | while | flops 1031795712 | bytes 81219784 | solution.py:222
  377.1 2.6 fusion.142
  379.7 2.3 multiply_reduce_fusion.10
  382.0 1.9 multiply_convert_fusion.5
  385.9 2.0 copy.222
  387.9 3.3 constant_dynamic-update-slice_fusion.5
  394.9 2.6 fusion.142
  397.5 2.3 multiply_reduce_fusion.10
  399.8 1.9 multiply_convert_fusion.5
  403.7 2.0 copy.222
  405.7 3.3 constant_dynamic-update-slice_fusion.5
  409.0 2.7 bitcast_convert_fusion.1
  411.7 1.4 copy-done.12
  413.2 3.4 bitcast_convert_fusion
  417.7 3.8 fusion.48
  421.5 19.6 %all-reduce.17.cloned.1.call-done = (bf16[1024,768]{1,0:T(8,128)(2,1)}, bf16[1024,768]{1,0:T(8,128)(2,1)}) async-done(((bf16[1024,768]{1,0:T(8,128)(2,1)}, bf16[1024,768]{1,0:T(8,128)(2,1)}), (bf16[1024,768]{1,0:T(8,128)(2,1)}, bf16[1024,768]{1,0:T(8,128)(2,1)})) %all-reduce.17.cloned.1.call-update) | async-done | bytes 3145744 | tf_op jit(solution)/shard_map/psum | solution.py:203
  441.2 2.9 fusion.40
  445.1 5.8 convolution_bitcast_fusion.1
  451.0 6.3 copy.167
  458.7 7.0 fusion.44
  465.7 9.5 fusion.51
  477.3 2.1 slice_reduce_fusion.1
  479.4 77.4 %all-reduce.4 = (f32[2,384]{1,0:T(2,128)S(1)}, f32[1536]{0:T(1024)S(1)}) all-reduce(f32[2,384]{1,0:T(2,128)S(1)} %pad_maximum_fusion, f32[1536]{0:T(1024)S(1)} %copy-done.34), channel_id=6, replica_groups=mesh['dp'=16,'mp'=2] {'dp'}, use_global_device_ids=true, to_apply=%region_31.32.clone | all-reduce | flops 2304 | bytes 18432
  558.2 14.1 %reduce-scatter.8.cloned.1.call-done = f32[24,768]{1,0:T(8,128)} async-done(((f32[384,768]{1,0:T(8,128)}), f32[24,768]{1,0:T(8,128)}) %reduce-scatter.8.cloned.1.call-update) | async-done | bytes 73744 | tf_op jit(solution)/shard_map/reduce_scatter | solution.py:253
  572.3 1.5 multiply_reduce_fusion.5
  573.8 124.7 %reduce-scatter.14.cloned.1.call-done = f32[48,6]{1,0:T(8,128)} async-done(((f32[768,6]{1,0:T(8,128)}), f32[48,6]{1,0:T(8,128)}) %reduce-scatter.14.cloned.1.call-update) | async-done | bytes 1168
  700.6 182.5 %all-reduce.15.cloned.1.call-done = f32[3,768,384]{2,0,1:T(4,128)} async-done(((f32[3,768,384]{2,0,1:T(4,128)}), f32[3,768,384]{2,0,1:T(4,128)}) %all-reduce.15.cloned.1.call-update) | async-done | bytes 3538960
  883.1 1.7 multiply_reduce_fusion.4
  886.2 139.5 %reduce-scatter.10.cloned.1.call-done = f32[48,1536]{1,0:T(8,128)} async-done(((f32[768,1536]{1,0:T(8,128)}), f32[48,1536]{1,0:T(8,128)}) %reduce-scatter.10.cloned.1.call-update) | async-done | bytes 294928 | tf_op jit(solution)/shard_map/reduce_scatter | solution.py:254
  1025.7 1.6 multiply_reduce_fusion.3
  1027.9 139.6 %reduce-scatter.12.cloned.1.call-done = f32[96,768]{1,0:T(8,128)} async-done(((f32[1536,768]{1,0:T(8,128)}), f32[96,768]{1,0:T(8,128)}) %reduce-scatter.12.cloned.1.call-update) | async-done | bytes 294928 | tf_op jit(solution)/shard_map/reduce_scatter | solution.py:255
  1167.5 1.6 multiply_reduce_fusion.2
  1171.2 5.1 fusion.31
  1176.4 39.8 %psum.39 = f32[]{:T(128)} all-reduce(f32[]{:T(128)S(6)} %add.327), channel_id=1, replica_groups=mesh['dp'=16,'mp'=2] {'dp','mp'}, use_global_device_ids=true, to_apply=%region_44.45 | all-reduce | flops 1 | bytes 8 | tf_op jit(solution)/shard_map/psum | solution.py:263
  1221.0 2.3 multiply_add_fusion.6
  1223.3 1.7 multiply_add_fusion.8
  1225.0 2.5 multiply_add_fusion.4
  (219 shorter events, 52.0 us)
Async XLA Ops:
  7.2 87.0 %copy-start = (bf16[1024,768]{1,0:T(8,128)(2,1)S(1)}, bf16[1024,768]{1,0:T(8,128)(2,1)}, u32[]{:S(2)}) copy-start(bf16[1024,768]{1,0:T(8,128)(2,1)} %param.36) | copy-start | bytes 4718596
  7.2 132.5 %all-gather.6.cloned.1.call-start = ((), (), s32[]{:S(2)}) async-start(), calls=%async_computation.4 | async-start | bytes 1880064 | tf_op jit(solution)/shard_map/all_gather | solution.py:161
  9.0 211.6 %all-reduce.11.cloned.1.call-start = ((), (), s32[]{:S(2)}) async-start(), calls=%async_computation.5 | async-start | bytes 3145728 | tf_op jit(solution)/shard_map/psum | solution.py:193
  91.7 52.0 %copy-start.29 = (f32[768]{0:T(1024)}, f32[768]{0:T(1024)S(1)}, u32[]{:S(2)}) copy-start(f32[768]{0:T(1024)S(1)} %get-tuple-element.328) | copy-start | bytes 9220
  91.7 52.0 %copy-start.38 = (f32[768]{0:T(1024)}, f32[768]{0:T(1024)S(1)}, u32[]{:S(2)}) copy-start(f32[768]{0:T(1024)S(1)} %get-tuple-element.327) | copy-start | bytes 9220
  94.3 49.5 %copy-start.25 = (f32[1024]{0:T(1024)}, f32[1024]{0:T(1024)S(1)}, u32[]{:S(2)}) copy-start(f32[1024]{0:T(1024)S(1)} %broadcast_multiply_fusion.5) | copy-start | bytes 12292
  94.9 48.9 %copy-start.27 = (f32[1024]{0:T(1024)}, f32[1024]{0:T(1024)S(1)}, u32[]{:S(2)}) copy-start(f32[1024]{0:T(1024)S(1)} %add_rsqrt_fusion.1) | copy-start | bytes 12292
  159.7 2.7 copy-start.22
  162.5 0.6 copy-start.23
  169.7 2.7 copy-start.22
  172.4 0.6 copy-start.23
  175.0 45.5 %copy-start.4 = (bf16[2,512,384]{1,2,0:T(8,128)(2,1)}, bf16[2,512,384]{1,2,0:T(8,128)(2,1)S(1)}, u32[]{:S(2)}) copy-start(bf16[2,512,384]{1,2,0:T(8,128)(2,1)S(1)} %get-tuple-element.594) | copy-start | bytes 2359300
  175.0 45.5 %copy-start.6 = (bf16[2,512,384]{1,2,0:T(8,128)(2,1)}, bf16[2,512,384]{1,2,0:T(8,128)(2,1)S(1)}, u32[]{:S(2)}) copy-start(bf16[2,512,384]{1,2,0:T(8,128)(2,1)S(1)} %get-tuple-element.595) | copy-start | bytes 2359300
  175.0 4.1 copy-start.14
  175.0 6.6 copy-start.42
  175.0 6.6 copy-start.40
  179.1 83.7 %all-gather.8.cloned.1.call-start = ((), (), s32[]{:S(2)}) async-start(), calls=%async_computation.6 | async-start | bytes 2506752 | tf_op jit(solution)/shard_map/all_gather | solution.py:163
  179.8 147.7 %all-gather.10.cloned.1.call-start = ((), (), s32[]{:S(2)}) async-start(), calls=%async_computation.7 | async-start | bytes 2506752 | tf_op jit(solution)/shard_map/all_gather | solution.py:164
  181.6 181.8 %all-reduce.13.cloned.1.call-start = ((), (), s32[]{:S(2)}) async-start(), calls=%async_computation.8 | async-start | bytes 3145728 | tf_op jit(solution)/shard_map/psum | solution.py:215
  220.6 2.1 copy-start.2
  220.6 42.2 %copy-start.36 = (f32[768]{0:T(1024)S(1)}, f32[768]{0:T(1024)}, u32[]{:S(2)}) copy-start(f32[768]{0:T(1024)} %get-tuple-element.324) | copy-start | bytes 9220
  262.8 64.7 %copy-start.33 = (f32[1536]{0:T(1024)S(1)}, f32[1536]{0:T(1024)}, u32[]{:S(2)}) copy-start(f32[1536]{0:T(1024)} %convert_element_type.158) | copy-start | bytes 18436
  327.5 12.8 %copy-start.44 = (bf16[768,1536]{1,0:T(8,128)(2,1)S(1)}, bf16[768,1536]{1,0:T(8,128)(2,1)}, u32[]{:S(2)}) copy-start(bf16[768,1536]{1,0:T(8,128)(2,1)} %all-gather.8.cloned.1.call-done) | copy-start | bytes 7077892
  338.6 1.7 copy-start.46
  344.0 97.1 %all-reduce.17.cloned.1.call-start = ((), (), s32[]{:S(2)}) async-start(), calls=%async_computation.14 | async-start | bytes 6291456 | tf_op jit(solution)/shard_map/psum | solution.py:203
  363.4 3.6 copy-start.10
  363.4 3.6 copy-start.13
  367.0 3.4 copy-start.11
  370.4 3.0 copy-start.5
  370.4 3.0 copy-start.24
  373.4 1.2 copy-start.8
  384.6 1.1 copy-start.7
  387.9 3.3 copy-start.9
  391.2 1.1 copy-start.8
  402.4 1.1 copy-start.7
  405.7 3.3 copy-start.9
  409.0 4.2 copy-start.45
  411.7 1.4 copy-start.12
  416.5 1.1 copy-start.17
  416.6 24.6 %copy-start.1 = (bf16[1024,768]{1,0:T(8,128)(2,1)S(1)}, bf16[1024,768]{1,0:T(8,128)(2,1)}, u32[]{:S(2)}) copy-start(bf16[1024,768]{1,0:T(8,128)(2,1)} %param.36) | copy-start | bytes 4718596
  416.6 24.6 %copy-start.26 = (f32[1024]{0:T(1024)S(1)}, f32[1024]{0:T(1024)}, u32[]{:S(2)}) copy-start(f32[1024]{0:T(1024)} %copy-done.25) | copy-start | bytes 12292
  416.6 24.6 %copy-start.28 = (f32[1024]{0:T(1024)S(1)}, f32[1024]{0:T(1024)}, u32[]{:S(2)}) copy-start(f32[1024]{0:T(1024)} %copy-done.27) | copy-start | bytes 12292
  416.6 24.6 %copy-start.30 = (f32[768]{0:T(1024)S(1)}, f32[768]{0:T(1024)}, u32[]{:S(2)}) copy-start(f32[768]{0:T(1024)} %copy-done.29) | copy-start | bytes 9220
  416.6 155.7 %reduce-scatter.8.cloned.1.call-start = ((), (), s32[]{:S(2)}) async-start(), calls=%async_computation.9 | async-start | bytes 1253376 | tf_op jit(solution)/shard_map/reduce_scatter | solution.py:253
  421.4 23.7 %copy-start.39 = (f32[768]{0:T(1024)S(1)}, f32[768]{0:T(1024)}, u32[]{:S(2)}) copy-start(f32[768]{0:T(1024)} %copy-done.38) | copy-start | bytes 9220
  421.4 277.1 %reduce-scatter.14.cloned.1.call-start = ((), (), s32[]{:S(2)}) async-start(), calls=%async_computation.12 | async-start | bytes 417792
  445.1 438.1 %all-reduce.15.cloned.1.call-start = ((), (), s32[]{:S(2)}) async-start(), calls=%async_computation.13 | async-start | bytes 9437184
  457.3 1.4 copy-start.3
  457.3 1.4 copy-start.37
  457.3 568.3 %reduce-scatter.10.cloned.1.call-start = ((), (), s32[]{:S(2)}) async-start(), calls=%async_computation.10 | async-start | bytes 5013504 | tf_op jit(solution)/shard_map/reduce_scatter | solution.py:254
  465.7 701.8 %reduce-scatter.12.cloned.1.call-start = ((), (), s32[]{:S(2)}) async-start(), calls=%async_computation.11 | async-start | bytes 5013504 | tf_op jit(solution)/shard_map/reduce_scatter | solution.py:255
  475.3 4.2 copy-start.34
  475.3 695.9 %copy-start.31 = (f32[768]{0:T(1024)S(1)}, f32[768]{0:T(1024)}, u32[]{:S(2)}) copy-start(f32[768]{0:T(1024)} %get-tuple-element.323) | copy-start | bytes 9220
  556.8 17.0 %copy-start.41 = (f32[2,384]{1,0:T(2,128)}, f32[2,384]{1,0:T(2,128)S(1)}, u32[]{:S(2)}) copy-start(f32[2,384]{1,0:T(2,128)S(1)} %get-tuple-element.361) | copy-start | bytes 9220
  556.8 143.8 %copy-start.43 = (f32[1536]{0:T(1024)}, f32[1536]{0:T(1024)S(1)}, u32[]{:S(2)}) copy-start(f32[1536]{0:T(1024)S(1)} %get-tuple-element.362) | copy-start | bytes 18436
  1171.1 48.5 %copy-start.32 = (f32[6,48]{1,0:T(8,128)S(1)}, f32[6,48]{1,0:T(8,128)}, u32[]{:S(2)}) copy-start(f32[6,48]{1,0:T(8,128)} %param.64) | copy-start | bytes 3460
  1171.2 48.5 %copy-start.35 = (f32[6,48]{1,0:T(8,128)S(1)}, f32[6,48]{1,0:T(8,128)}, u32[]{:S(2)}) copy-start(f32[6,48]{1,0:T(8,128)} %param.67) | copy-start | bytes 3460
  1171.2 52.1 %copy-start.18 = (f32[24,768]{1,0:T(8,128)S(1)}, f32[24,768]{1,0:T(8,128)}, u32[]{:S(2)}) copy-start(f32[24,768]{1,0:T(8,128)} %param.44) | copy-start | bytes 221188
  1176.3 51.2 %copy-start.15 = (f32[96,768]{1,0:T(8,128)S(1)}, f32[96,768]{1,0:T(8,128)}, u32[]{:S(2)}) copy-start(f32[96,768]{1,0:T(8,128)} %param.52) | copy-start | bytes 884740
  1176.3 51.2 %copy-start.16 = (f32[96,768]{1,0:T(8,128)S(1)}, f32[96,768]{1,0:T(8,128)}, u32[]{:S(2)}) copy-start(f32[96,768]{1,0:T(8,128)} %reduce-scatter.12.cloned.1.call-done) | copy-start | bytes 884740
  1176.3 51.2 %copy-start.19 = (f32[96,768]{1,0:T(8,128)S(1)}, f32[96,768]{1,0:T(8,128)}, u32[]{:S(2)}) copy-start(f32[96,768]{1,0:T(8,128)} %param.55) | copy-start | bytes 884740
  1176.3 51.2 %copy-start.20 = (f32[96,768]{1,0:T(8,128)S(1)}, f32[96,768]{1,0:T(8,128)}, u32[]{:S(2)}) copy-start(f32[96,768]{1,0:T(8,128)} %param.54) | copy-start | bytes 884740
  1176.4 51.2 %copy-start.21 = (f32[96,768]{1,0:T(8,128)S(1)}, f32[96,768]{1,0:T(8,128)}, u32[]{:S(2)}) copy-start(f32[96,768]{1,0:T(8,128)} %param.53) | copy-start | bytes 884740
Sparse Core Ops, SparseCore 0:
  11.3 61.8 all-gather.5
  179.2 16.2 all-reduce.10
  199.3 63.4 all-gather.7
  266.4 61.0 all-gather.9
  344.2 19.1 all-reduce.12
  416.7 24.4 all-reduce.16
  446.6 125.6 reduce-scatter.7
  578.2 120.2 reduce-scatter.13
  704.3 178.8 all-reduce.14
  889.0 136.6 reduce-scatter.9
  1030.8 136.6 reduce-scatter.11
where the time goes:
time: 1250 us; the launch traced here: 1240 us
  waiting for transfers between devices  728 us (58%)
  blocking collectives  275 us (22%)
  matrix products  93.5 us (7%)
  other arithmetic  65.3 us (5%)
  local copies, waits for them, and re-layouts  49.3 us (4%)
  between operations  23.7 us (2%)
    unnamed x13, waiting for transfers between devices  307 us
    reduce_scatter x1, waiting for transfers between devices, body(): lax.psum_scatter(grad_down, 'dp', scatter_dimension=0, tiled=True)  140 us
    reduce_scatter x1, waiting for transfers between devices, body(): lax.psum_scatter(grad_up, 'dp', scatter_dimension=0, tiled=True)  139 us
    unnamed x2, blocking collectives  114 us
    all_gather x1, waiting for transfers between devices, body(): lax.all_gather(down_weight.astype(bfloat), 'dp', axis=0, tiled=True)  58.1 us
    all_gather x1, blocking collectives, body(): lax.all_gather(attn_weight.astype(bfloat), 'dp', axis=0, tiled=True)  43.5 us
    all_gather x1, blocking collectives, body(): lax.all_gather(head_bias.astype(bfloat), 'dp', axis=1, tiled=True)  42.2 us
    psum x1, blocking collectives, body(): grad_norm = jnp.sqrt(lax.psum(squares_local, ('dp', 'mp')))  39.8 us
  transfers between devices with their start and end apart: 11, of which 9 were waited for; matrix products, arithmetic and copies ran while one was open for 6% of the time, Pallas kernels for 0%

commit v1 on v0

--- a/solution.py
+++ b/solution.py
@@ -260,7 +260,7 @@
     squares_local = sum((jnp.sum(member * member) for member in reduced[:6])) + 0.5 * jnp.sum(
         reduced[6] * reduced[6]
     )
-    grad_norm = jnp.sqrt(lax.psum(squares_local, ("dp", "mp")))
+    grad_norm = jnp.sqrt(lax.psum(lax.psum(squares_local, "mp"), "dp"))
     factor = CLIP_NORM / jnp.maximum(grad_norm, CLIP_NORM)
     moment_qkv, square_qkv, updated_qkv, smooth_qkv = adam_step(
         reduced[0], qkv_weight, first_qkv, second_qkv, average_qkv, factor, WEIGHT_DECAY, LEARN_RATE

time: 1250 us -> 1250 us (level)
    psum x1 -> x2, blocking collectives: 39.8 us -> 43.3 us  [body(): grad_norm = jnp.sqrt(lax.psum(lax.psum(squares_local, 'mp'), 'dp'))]
where the time goes in v1:
time: 1250 us; the launch traced here: 1240 us
  waiting for transfers between devices  728 us (58%)
  blocking collectives  279 us (22%)
  matrix products  93.5 us (7%)
  other arithmetic  65.3 us (5%)
  local copies, waits for them, and re-layouts  49.3 us (4%)
  between operations  23.7 us (2%)
    unnamed x13, waiting for transfers between devices  307 us
    reduce_scatter x1, waiting for transfers between devices, body(): lax.psum_scatter(grad_down, 'dp', scatter_dimension=0, tiled=True)  140 us
    reduce_scatter x1, waiting for transfers between devices, body(): lax.psum_scatter(grad_up, 'dp', scatter_dimension=0, tiled=True)  139 us
    unnamed x2, blocking collectives  114 us
    all_gather x1, waiting for transfers between devices, body(): lax.all_gather(down_weight.astype(bfloat), 'dp', axis=0, tiled=True)  58.1 us
    all_gather x1, blocking collectives, body(): lax.all_gather(attn_weight.astype(bfloat), 'dp', axis=0, tiled=True)  43.5 us
    psum x2, blocking collectives, body(): grad_norm = jnp.sqrt(lax.psum(lax.psum(squares_local, 'mp'), 'dp'))  43.3 us
    all_gather x1, blocking collectives, body(): lax.all_gather(head_bias.astype(bfloat), 'dp', axis=1, tiled=True)  42.2 us
  transfers between devices with their start and end apart: 11, of which 9 were waited for; matrix products, arithmetic and copies ran while one was open for 6% of the time, Pallas kernels for 0%

profile of v1, /device:TPU:0, one launch (start us, length us, event | category | flops | bytes accessed | tf_op | source)
XLA Modules:
  0.0 1240.1 jit_solution(14195529249144815473)
XLA Ops:
  7.3 1.7 convert_element_type.145
  10.6 42.2 %all-gather.1 = bf16[16,24,2]{1,2,0:T(2,128)(2,1)S(1)} all-gather(bf16[1,24,2]{1,2,0:T(2,128)(2,1)S(1)} %convert_bitcast_fusion.1), channel_id=1, replica_groups=mesh['dp'=16,'mp'=2] {'dp'}, dimensions={0}, use_global_device_ids=true | all-gather | bytes 1632 | tf_op jit(solution)/shard_map/all_gather | solution.py:165
  53.6 35.9 %all-gather = bf16[16,48,6]{1,2,0:T(8,128)(2,1)S(1)} all-gather(bf16[1,48,6]{1,2,0:T(8,128)(2,1)S(1)} %convert_bitcast_fusion), channel_id=1, replica_groups=mesh['dp'=16,'mp'=2] {'dp'}, dimensions={0}, use_global_device_ids=true | all-gather | bytes 9792 | tf_op jit(solution)/shard_map/all_gather | solution.py:167
  91.8 1.7 convert_reduce_fusion.2
  96.2 43.5 %all_gather.24 = bf16[384,768]{1,0:T(8,128)(2,1)} all-gather(bf16[24,768]{1,0:T(8,128)(2,1)S(1)} %convert_element_type.152), channel_id=1, replica_groups=mesh['dp'=16,'mp'=2] {'dp'}, dimensions={0}, use_global_device_ids=true | all-gather | bytes 626688 | tf_op jit(solution)/shard_map/all_gather | solution.py:162
  139.8 4.0 convolution_bitcast_fusion
  146.1 3.0 copy.160
  149.2 1.6 copy.159
  152.2 3.0 add_convert_fusion.2
  155.2 19.9 %while.22 = (s32[]{:T(128)}, bf16[2,512,384]{2,1,0:T(8,128)(2,1)}, f32[2,6,512]{2,1,0:T(8,128)}, bf16[2,512,384]{1,2,0:T(8,128)(2,1)}, pred[2,512,512]{1,2,0:T(8...) while((s32[]{:T(128)}, bf16[2,512,384]{2,1,0:T(8,128)(2,1)}, ...), condition=%wide.region_7.8_spmd, body=%wide.region_4.7_spmd.sunk | while | flops 421721088 | bytes 25997480 | solution.py:186
  159.8 2.7 fusion.130
  169.7 2.7 fusion.130
  175.1 4.0 convolution_convert_fusion
  179.9 1.7 convert_element_type.160
  183.2 36.7 %all-reduce = bf16[1536]{0:T(1024)(128)(2,1)S(1)} all-reduce(bf16[1536]{0:T(1024)(128)(2,1)S(1)} %dynamic-update-slice), channel_id=1, replica_groups=mesh['dp'=16,'mp'=2] {'dp'}, use_global_device_ids=true, to_apply=%add | all-reduce | flops 1536 | bytes 6144
  220.6 2.1 fusion.47
  223.6 39.2 %all-gather.8.cloned.1.call-done = bf16[768,1536]{1,0:T(8,128)(2,1)} async-done(((bf16[48,1536]{1,0:T(8,128)(2,1)}), bf16[768,1536]{1,0:T(8,128)(2,1)}) %all-gather.8.cloned.1.call-update) | async-done | bytes 2359312 | tf_op jit(solution)/shard_map/all_gather | solution.py:163
  262.8 6.6 fusion.67
  269.4 58.1 %all-gather.10.cloned.1.call-done = bf16[1536,768]{1,0:T(8,128)(2,1)} async-done(((bf16[96,768]{1,0:T(8,128)(2,1)}), bf16[1536,768]{1,0:T(8,128)(2,1)}) %all-gather.10.cloned.1.call-update) | async-done | bytes 2359312 | tf_op jit(solution)/shard_map/all_gather | solution.py:164
  327.5 11.1 fusion.79
  338.6 1.7 copy-done.46
  340.3 3.7 convolution_convert_fusion.1
  344.1 8.6 convolution_convert_fusion.2
  352.7 10.7 all-reduce.13.cloned.1.call-done
  363.4 3.5 fusion.39
  367.0 3.4 fusion.75
  370.4 3.0 convolution_convert_fusion.3
  373.3 35.6 %while.23 = (s32[]{:T(128)}, f32[2,3,512,384]{3,2,0,1:T(8,128)}, bf16[2,512,384]{1,2,0:T(8,128)(2,1)S(1)}, pred[2,512,512]{1,2,0:T(8,128)(4,1)}, bf16[2,512,384]...) while((s32[]{:T(128)}, f32[2,3,512,384]{3,2,0,1:T(8,128)}, ...), condition=%wide.region_17.18_spmd, body=%wide.region_15.17_spmd.sunk | while | flops 1031795712 | bytes 81219784 | solution.py:222
  377.1 2.6 fusion.142
  379.7 2.3 multiply_reduce_fusion.10
  382.0 1.9 multiply_convert_fusion.5
  385.9 2.0 copy.222
  387.9 3.3 constant_dynamic-update-slice_fusion.5
  394.8 2.6 fusion.142
  397.5 2.3 multiply_reduce_fusion.10
  399.8 1.9 multiply_convert_fusion.5
  403.7 2.0 copy.222
  405.7 3.3 constant_dynamic-update-slice_fusion.5
  409.0 2.7 bitcast_convert_fusion.1
  413.1 3.4 bitcast_convert_fusion
  417.6 3.8 fusion.48
  421.5 19.6 %all-reduce.17.cloned.1.call-done = (bf16[1024,768]{1,0:T(8,128)(2,1)}, bf16[1024,768]{1,0:T(8,128)(2,1)}) async-done(((bf16[1024,768]{1,0:T(8,128)(2,1)}, bf16[1024,768]{1,0:T(8,128)(2,1)}), (bf16[1024,768]{1,0:T(8,128)(2,1)}, bf16[1024,768]{1,0:T(8,128)(2,1)})) %all-reduce.17.cloned.1.call-update) | async-done | bytes 3145744 | tf_op jit(solution)/shard_map/psum | solution.py:203
  441.1 2.9 fusion.40
  445.1 5.8 convolution_bitcast_fusion.1
  450.9 6.3 copy.167
  458.7 7.0 fusion.44
  465.7 9.5 fusion.51
  477.3 2.1 slice_reduce_fusion.1
  479.4 77.4 %all-reduce.4 = (f32[2,384]{1,0:T(2,128)S(1)}, f32[1536]{0:T(1024)S(1)}) all-reduce(f32[2,384]{1,0:T(2,128)S(1)} %pad_maximum_fusion, f32[1536]{0:T(1024)S(1)} %copy-done.34), channel_id=6, replica_groups=mesh['dp'=16,'mp'=2] {'dp'}, use_global_device_ids=true, to_apply=%region_31.32.clone | all-reduce | flops 2304 | bytes 18432
  558.2 14.1 %reduce-scatter.8.cloned.1.call-done = f32[24,768]{1,0:T(8,128)} async-done(((f32[384,768]{1,0:T(8,128)}), f32[24,768]{1,0:T(8,128)}) %reduce-scatter.8.cloned.1.call-update) | async-done | bytes 73744 | tf_op jit(solution)/shard_map/reduce_scatter | solution.py:253
  572.3 1.5 multiply_reduce_fusion.5
  573.8 124.7 %reduce-scatter.14.cloned.1.call-done = f32[48,6]{1,0:T(8,128)} async-done(((f32[768,6]{1,0:T(8,128)}), f32[48,6]{1,0:T(8,128)}) %reduce-scatter.14.cloned.1.call-update) | async-done | bytes 1168
  700.6 182.5 %all-reduce.15.cloned.1.call-done = f32[3,768,384]{2,0,1:T(4,128)} async-done(((f32[3,768,384]{2,0,1:T(4,128)}), f32[3,768,384]{2,0,1:T(4,128)}) %all-reduce.15.cloned.1.call-update) | async-done | bytes 3538960
  883.1 1.7 multiply_reduce_fusion.4
  886.1 139.5 %reduce-scatter.10.cloned.1.call-done = f32[48,1536]{1,0:T(8,128)} async-done(((f32[768,1536]{1,0:T(8,128)}), f32[48,1536]{1,0:T(8,128)}) %reduce-scatter.10.cloned.1.call-update) | async-done | bytes 294928 | tf_op jit(solution)/shard_map/reduce_scatter | solution.py:254
  1025.6 1.6 multiply_reduce_fusion.3
  1027.9 139.6 %reduce-scatter.12.cloned.1.call-done = f32[96,768]{1,0:T(8,128)} async-done(((f32[1536,768]{1,0:T(8,128)}), f32[96,768]{1,0:T(8,128)}) %reduce-scatter.12.cloned.1.call-update) | async-done | bytes 294928 | tf_op jit(solution)/shard_map/reduce_scatter | solution.py:255
  1167.5 1.6 multiply_reduce_fusion.2
  1171.1 3.0 psum.46
  1174.1 5.1 fusion.31
  1179.3 40.4 %psum.47 = f32[]{:T(128)} all-reduce(f32[]{:T(128)} %psum.46), channel_id=1, replica_groups=mesh['dp'=16,'mp'=2] {'dp'}, use_global_device_ids=true, to_apply=%region_45.46 | all-reduce | flops 1 | bytes 8 | tf_op jit(solution)/shard_map/psum | solution.py:263
  1224.5 2.3 multiply_add_fusion.6
  1226.8 1.7 multiply_add_fusion.8
  1228.5 2.5 multiply_add_fusion.4
  (220 shorter events, 53.4 us)
Async XLA Ops:
  7.2 87.0 %copy-start = (bf16[1024,768]{1,0:T(8,128)(2,1)S(1)}, bf16[1024,768]{1,0:T(8,128)(2,1)}, u32[]{:S(2)}) copy-start(bf16[1024,768]{1,0:T(8,128)(2,1)} %param.36) | copy-start | bytes 4718596
  7.2 132.5 %all-gather.6.cloned.1.call-start = ((), (), s32[]{:S(2)}) async-start(), calls=%async_computation.4 | async-start | bytes 1880064 | tf_op jit(solution)/shard_map/all_gather | solution.py:161
  9.0 211.6 %all-reduce.11.cloned.1.call-start = ((), (), s32[]{:S(2)}) async-start(), calls=%async_computation.5 | async-start | bytes 3145728 | tf_op jit(solution)/shard_map/psum | solution.py:193
  91.7 52.0 %copy-start.29 = (f32[768]{0:T(1024)}, f32[768]{0:T(1024)S(1)}, u32[]{:S(2)}) copy-start(f32[768]{0:T(1024)S(1)} %get-tuple-element.328) | copy-start | bytes 9220
  91.7 52.0 %copy-start.38 = (f32[768]{0:T(1024)}, f32[768]{0:T(1024)S(1)}, u32[]{:S(2)}) copy-start(f32[768]{0:T(1024)S(1)} %get-tuple-element.327) | copy-start | bytes 9220
  94.3 49.5 %copy-start.25 = (f32[1024]{0:T(1024)}, f32[1024]{0:T(1024)S(1)}, u32[]{:S(2)}) copy-start(f32[1024]{0:T(1024)S(1)} %broadcast_multiply_fusion.5) | copy-start | bytes 12292
  94.9 48.9 %copy-start.27 = (f32[1024]{0:T(1024)}, f32[1024]{0:T(1024)S(1)}, u32[]{:S(2)}) copy-start(f32[1024]{0:T(1024)S(1)} %add_rsqrt_fusion.1) | copy-start | bytes 12292
  159.7 2.7 copy-start.22
  162.5 0.6 copy-start.23
  169.7 2.7 copy-start.22
  172.4 0.6 copy-start.23
  175.0 45.5 %copy-start.4 = (bf16[2,512,384]{1,2,0:T(8,128)(2,1)}, bf16[2,512,384]{1,2,0:T(8,128)(2,1)S(1)}, u32[]{:S(2)}) copy-start(bf16[2,512,384]{1,2,0:T(8,128)(2,1)S(1)} %get-tuple-element.594) | copy-start | bytes 2359300
  175.0 45.5 %copy-start.6 = (bf16[2,512,384]{1,2,0:T(8,128)(2,1)}, bf16[2,512,384]{1,2,0:T(8,128)(2,1)S(1)}, u32[]{:S(2)}) copy-start(bf16[2,512,384]{1,2,0:T(8,128)(2,1)S(1)} %get-tuple-element.595) | copy-start | bytes 2359300
  175.0 4.1 copy-start.14
  175.0 6.6 copy-start.42
  175.0 6.6 copy-start.40
  179.1 83.7 %all-gather.8.cloned.1.call-start = ((), (), s32[]{:S(2)}) async-start(), calls=%async_computation.6 | async-start | bytes 2506752 | tf_op jit(solution)/shard_map/all_gather | solution.py:163
  179.8 147.7 %all-gather.10.cloned.1.call-start = ((), (), s32[]{:S(2)}) async-start(), calls=%async_computation.7 | async-start | bytes 2506752 | tf_op jit(solution)/shard_map/all_gather | solution.py:164
  181.6 181.8 %all-reduce.13.cloned.1.call-start = ((), (), s32[]{:S(2)}) async-start(), calls=%async_computation.8 | async-start | bytes 3145728 | tf_op jit(solution)/shard_map/psum | solution.py:215
  220.6 2.1 copy-start.2
  220.6 42.2 %copy-start.36 = (f32[768]{0:T(1024)S(1)}, f32[768]{0:T(1024)}, u32[]{:S(2)}) copy-start(f32[768]{0:T(1024)} %get-tuple-element.324) | copy-start | bytes 9220
  262.8 64.7 %copy-start.33 = (f32[1536]{0:T(1024)S(1)}, f32[1536]{0:T(1024)}, u32[]{:S(2)}) copy-start(f32[1536]{0:T(1024)} %convert_element_type.158) | copy-start | bytes 18436
  327.5 12.8 %copy-start.44 = (bf16[768,1536]{1,0:T(8,128)(2,1)S(1)}, bf16[768,1536]{1,0:T(8,128)(2,1)}, u32[]{:S(2)}) copy-start(bf16[768,1536]{1,0:T(8,128)(2,1)} %all-gather.8.cloned.1.call-done) | copy-start | bytes 7077892
  338.6 1.7 copy-start.46
  344.0 97.1 %all-reduce.17.cloned.1.call-start = ((), (), s32[]{:S(2)}) async-start(), calls=%async_computation.14 | async-start | bytes 6291456 | tf_op jit(solution)/shard_map/psum | solution.py:203
  363.4 3.6 copy-start.10
  363.4 3.6 copy-start.13
  367.0 3.4 copy-start.11
  370.4 3.0 copy-start.5
  370.4 3.0 copy-start.24
  373.4 1.2 copy-start.8
  384.6 1.1 copy-start.7
  387.9 3.3 copy-start.9
  391.2 1.1 copy-start.8
  402.3 1.1 copy-start.7
  405.7 3.3 copy-start.9
  409.0 4.2 copy-start.45
  411.7 1.4 copy-start.12
  416.5 1.1 copy-start.17
  416.5 24.6 %copy-start.1 = (bf16[1024,768]{1,0:T(8,128)(2,1)S(1)}, bf16[1024,768]{1,0:T(8,128)(2,1)}, u32[]{:S(2)}) copy-start(bf16[1024,768]{1,0:T(8,128)(2,1)} %param.36) | copy-start | bytes 4718596
  416.5 24.6 %copy-start.26 = (f32[1024]{0:T(1024)S(1)}, f32[1024]{0:T(1024)}, u32[]{:S(2)}) copy-start(f32[1024]{0:T(1024)} %copy-done.25) | copy-start | bytes 12292
  416.6 24.6 %copy-start.28 = (f32[1024]{0:T(1024)S(1)}, f32[1024]{0:T(1024)}, u32[]{:S(2)}) copy-start(f32[1024]{0:T(1024)} %copy-done.27) | copy-start | bytes 12292
  416.6 24.6 %copy-start.30 = (f32[768]{0:T(1024)S(1)}, f32[768]{0:T(1024)}, u32[]{:S(2)}) copy-start(f32[768]{0:T(1024)} %copy-done.29) | copy-start | bytes 9220
  416.6 155.7 %reduce-scatter.8.cloned.1.call-start = ((), (), s32[]{:S(2)}) async-start(), calls=%async_computation.9 | async-start | bytes 1253376 | tf_op jit(solution)/shard_map/reduce_scatter | solution.py:253
  421.4 23.7 %copy-start.39 = (f32[768]{0:T(1024)S(1)}, f32[768]{0:T(1024)}, u32[]{:S(2)}) copy-start(f32[768]{0:T(1024)} %copy-done.38) | copy-start | bytes 9220
  421.4 277.1 %reduce-scatter.14.cloned.1.call-start = ((), (), s32[]{:S(2)}) async-start(), calls=%async_computation.12 | async-start | bytes 417792
  445.1 438.1 %all-reduce.15.cloned.1.call-start = ((), (), s32[]{:S(2)}) async-start(), calls=%async_computation.13 | async-start | bytes 9437184
  457.3 1.4 copy-start.3
  457.3 1.4 copy-start.37
  457.3 568.3 %reduce-scatter.10.cloned.1.call-start = ((), (), s32[]{:S(2)}) async-start(), calls=%async_computation.10 | async-start | bytes 5013504 | tf_op jit(solution)/shard_map/reduce_scatter | solution.py:254
  465.7 701.9 %reduce-scatter.12.cloned.1.call-start = ((), (), s32[]{:S(2)}) async-start(), calls=%async_computation.11 | async-start | bytes 5013504 | tf_op jit(solution)/shard_map/reduce_scatter | solution.py:255
  475.3 4.2 copy-start.34
  475.3 698.8 %copy-start.31 = (f32[768]{0:T(1024)S(1)}, f32[768]{0:T(1024)}, u32[]{:S(2)}) copy-start(f32[768]{0:T(1024)} %get-tuple-element.323) | copy-start | bytes 9220
  556.8 17.0 %copy-start.41 = (f32[2,384]{1,0:T(2,128)}, f32[2,384]{1,0:T(2,128)S(1)}, u32[]{:S(2)}) copy-start(f32[2,384]{1,0:T(2,128)S(1)} %get-tuple-element.361) | copy-start | bytes 9220
  556.8 617.3 %copy-start.43 = (f32[1536]{0:T(1024)}, f32[1536]{0:T(1024)S(1)}, u32[]{:S(2)}) copy-start(f32[1536]{0:T(1024)S(1)} %get-tuple-element.362) | copy-start | bytes 18436
  1174.1 49.1 %copy-start.32 = (f32[6,48]{1,0:T(8,128)S(1)}, f32[6,48]{1,0:T(8,128)}, u32[]{:S(2)}) copy-start(f32[6,48]{1,0:T(8,128)} %param.64) | copy-start | bytes 3460
  1174.1 49.1 %copy-start.35 = (f32[6,48]{1,0:T(8,128)S(1)}, f32[6,48]{1,0:T(8,128)}, u32[]{:S(2)}) copy-start(f32[6,48]{1,0:T(8,128)} %param.67) | copy-start | bytes 3460
  1174.1 52.7 %copy-start.18 = (f32[24,768]{1,0:T(8,128)S(1)}, f32[24,768]{1,0:T(8,128)}, u32[]{:S(2)}) copy-start(f32[24,768]{1,0:T(8,128)} %param.44) | copy-start | bytes 221188
  1179.3 51.8 %copy-start.15 = (f32[96,768]{1,0:T(8,128)S(1)}, f32[96,768]{1,0:T(8,128)}, u32[]{:S(2)}) copy-start(f32[96,768]{1,0:T(8,128)} %param.52) | copy-start | bytes 884740
  1179.3 51.8 %copy-start.16 = (f32[96,768]{1,0:T(8,128)S(1)}, f32[96,768]{1,0:T(8,128)}, u32[]{:S(2)}) copy-start(f32[96,768]{1,0:T(8,128)} %reduce-scatter.12.cloned.1.call-done) | copy-start | bytes 884740
  1179.3 51.8 %copy-start.19 = (f32[96,768]{1,0:T(8,128)S(1)}, f32[96,768]{1,0:T(8,128)}, u32[]{:S(2)}) copy-start(f32[96,768]{1,0:T(8,128)} %param.55) | copy-start | bytes 884740
  1179.3 51.8 %copy-start.20 = (f32[96,768]{1,0:T(8,128)S(1)}, f32[96,768]{1,0:T(8,128)}, u32[]{:S(2)}) copy-start(f32[96,768]{1,0:T(8,128)} %param.54) | copy-start | bytes 884740
  1179.3 51.8 %copy-start.21 = (f32[96,768]{1,0:T(8,128)S(1)}, f32[96,768]{1,0:T(8,128)}, u32[]{:S(2)}) copy-start(f32[96,768]{1,0:T(8,128)} %param.53) | copy-start | bytes 884740
Sparse Core Ops, SparseCore 0:
  11.3 61.8 all-gather.5
  179.2 16.2 all-reduce.10
  199.3 63.4 all-gather.7
  266.4 61.0 all-gather.9
  344.1 19.1 all-reduce.12
  416.6 24.4 all-reduce.16
  446.6 125.6 reduce-scatter.7
  578.2 120.2 reduce-scatter.13
  704.2 178.8 all-reduce.14
  889.0 136.6 reduce-scatter.9
  1030.8 136.6 reduce-scatter.11
